TPU v7x, 512 devices: a whole 4x4x16 slice. The times are simulated.
512 devices in a mesh: fsdp: 16 (over z), replica: 16 (over x_lo, y, core), tm: 2 (over x_hi).
Axes of the slice: x: 4 (x_hi: 2, x_lo: 2; x = x_hi * 2 + x_lo), y: 4, z: 16, core: 2. Of those that a mesh axis runs over, the one named last changes fastest.
Arguments:
- clip_input: bfloat16 [16, 8, 16, 16, 512], P('replica', 'tm'), may hold values from -6 to 6
- first_kernel: bfloat16 [27, 512, 512], P(None, None, 'fsdp'), may hold values from -0.0546875 to 0.0546875
- second_kernel: bfloat16 [27, 512, 512], P(None, 'fsdp'), may hold values from -0.0546875 to 0.0546875
- out_grad: bfloat16 [16, 2, 4, 4, 512], P('replica', 'tm'), may hold values from -1 to 1
- tap_mix: float32 [2, 27, 27], replicated, may hold values from -0.14 to 1.4
- left_panels: float32 [2, 512, 512], P(None, 'fsdp'), may hold values from -0.05 to 2
- right_panels: float32 [2, 512, 512], P(None, 'fsdp', ('replica', 'tm')), may hold values from -0.05 to 2
Outputs:
- update: bfloat16 [2, 27, 512, 512], P(None, None, 'fsdp', ('replica', 'tm'))
All inputs are finite; a program needn't handle non-finite values.
Results may differ from a plain program's by a relative error of at most 0.0049.
Values may be sent and summed in bfloat16 or wider, within the bound.
A program may use at most 128 MiB of HBM per device.

v0:
```python
import jax
import jax.numpy as jnp
from jax import lax
from jax.sharding import PartitionSpec as P

TAPS = 27


def shifted(block, axis, distance):
    devices = range(lax.axis_size(axis))
    route = [(i - distance, i) for i in devices if i - distance in devices]
    return lax.ppermute(block, axis, route)


def tap_patches(padded, out_frames, out_side):
    pieces_list = []
    for tap_index in range(TAPS):
        along_time = tap_index // 9
        along_rows = tap_index // 3 % 3
        along_cols = tap_index % 3
        pieces_list.append(
            padded[
                :,
                along_time : along_time + 2 * out_frames : 2,
                along_rows : along_rows + 2 * out_side : 2,
                along_cols : along_cols + 2 * out_side : 2,
                :,
            ]
        )
    return jnp.concatenate(pieces_list, axis=-1)


def spread_back(grad_shape, columns, out_frames, out_side, channels):
    total = jnp.zeros(grad_shape, jnp.float32)
    for tap_index in range(TAPS):
        along_time = tap_index // 9
        along_rows = tap_index // 3 % 3
        along_cols = tap_index % 3
        total = total.at[
            :,
            along_time : along_time + 2 * out_frames : 2,
            along_rows : along_rows + 2 * out_side : 2,
            along_cols : along_cols + 2 * out_side : 2,
            :,
        ].add(columns[..., tap_index * channels : (tap_index + 1) * channels])
    return total


def shards(clip_input, first_kernel, second_kernel, out_grad, tap_mix, left_panels, right_panels):
    highest = lax.Precision.HIGHEST
    clip_count = clip_input.shape[0]
    frames = clip_input.shape[1]
    side_cells = clip_input.shape[2]
    channels = clip_input.shape[4]
    own_width = first_kernel.shape[2]
    half_frames = frames // 2
    half_side = side_cells // 2
    quarter_frames = frames // 4
    quarter_side = side_cells // 4
    spatial_pad = ((0, 0), (0, 0), (1, 0), (1, 0), (0, 0))
    flat_kernel = first_kernel.reshape(TAPS * channels, own_width)
    prior_frame = shifted(clip_input[:, frames - 1 :], "tm", 1)
    extended = jnp.concatenate([prior_frame, clip_input], axis=1)
    padded_input = jnp.pad(extended, spatial_pad)
    first_patches = tap_patches(padded_input, half_frames, half_side).reshape(-1, TAPS * channels)
    pre_act = jnp.dot(first_patches, flat_kernel, preferred_element_type=jnp.float32)
    hidden = (
        jax.nn.silu(pre_act)
        .astype(jnp.bfloat16)
        .reshape(clip_count, half_frames, half_side, half_side, own_width)
    )
    prior_hidden = shifted(hidden[:, half_frames - 1 :], "tm", 1)
    padded_hidden = jnp.pad(jnp.concatenate([prior_hidden, hidden], axis=1), spatial_pad)
    second_patches = tap_patches(padded_hidden, quarter_frames, quarter_side).reshape(
        -1, TAPS * own_width
    )
    grad_rows = out_grad.reshape(-1, channels)
    second_grad = jnp.dot(grad_rows.T, second_patches, preferred_element_type=jnp.float32)
    second_grad = second_grad.reshape(channels, TAPS, own_width).transpose(1, 0, 2)
    back_columns = jnp.dot(
        grad_rows,
        second_kernel.reshape(TAPS * own_width, channels).T,
        preferred_element_type=jnp.float32,
    )
    back_columns = back_columns.reshape(
        clip_count, quarter_frames, quarter_side, quarter_side, TAPS * own_width
    )
    spread = spread_back(padded_hidden.shape, back_columns, quarter_frames, quarter_side, own_width)
    returned = shifted(spread[:, :1, 1:, 1:, :], "tm", -1)
    hidden_grad = spread[:, 1:, 1:, 1:, :]
    hidden_grad = hidden_grad.at[:, half_frames - 1 :].add(returned).reshape(-1, own_width)
    sigmoid_vals = jax.nn.sigmoid(pre_act)
    pre_grad = (hidden_grad * sigmoid_vals * (1.0 + pre_act * (1.0 - sigmoid_vals))).astype(
        jnp.bfloat16
    )
    first_grad = jnp.dot(first_patches.T, pre_grad, preferred_element_type=jnp.float32).reshape(
        TAPS, channels, own_width
    )
    stacked = jnp.stack([first_grad, second_grad])
    summed = lax.psum(stacked, ("replica", "tm"))
    tap_mixed = jnp.einsum("lst,ltij->lsij", tap_mix, summed, precision=highest)
    left_done = jnp.einsum(
        "lik,lskj->lsij",
        lax.all_gather(left_panels, "fsdp", axis=1, tiled=True),
        tap_mixed,
        precision=highest,
    )
    result = lax.psum_scatter(
        jnp.einsum("lsij,ljk->ilsk", left_done, right_panels, precision=highest),
        "fsdp",
        scatter_dimension=0,
        tiled=True,
    ).transpose(1, 2, 0, 3)
    return result.astype(jnp.bfloat16)


def solution(mesh):
    in_specs = (
        P("replica", "tm", None, None, None),
        P(None, None, "fsdp"),
        P(None, "fsdp", None),
        P("replica", "tm", None, None, None),
        P(),
        P(None, "fsdp", None),
        P(None, "fsdp", ("replica", "tm")),
    )
    out_specs = P(None, None, "fsdp", ("replica", "tm"))
    return jax.shard_map(shards, mesh=mesh, in_specs=in_specs, out_specs=out_specs, check_vma=False)
```

profile of v0, /device:TPU:4, one launch (start us, length us, event | category | flops | bytes accessed | tf_op | source)
XLA Modules:
  0.0 490.1 jit_solution(18250001880252223688)
XLA Ops:
  55.4 7.8 %collective-permute-start.1 = (f32[1,1,8,8,32]{4,1,3,2,0:T(1,128)S(1)}, f32[1,1,8,8,32]{4,1,3,2,0:T(1,128)S(1)}, u32[]{:S(2)}, u32[]{:S(2)}) collective-permute-start(f32[1,1,8,8,32]{4,1,3,2,0:T(1,128)S(1)} %slice.702), channel_id=1, source_target_pairs={{1,0},{3,2},{5,4},{7,6},{9,8},{11,10},{13,12},{15,14},{17,16},{19,... | collective-permute-start | bytes 24584 | tf_op jit(solution)/shard_map/ppermute | solution.py:12
  67.2 5.0 %slice.318 = bf16[1,2,8,8,512]{4,3,2,1,0:T(8,128)(2,1)} slice(bf16[1,5,17,17,512]{4,3,2,1,0:T(8,128)(2,1)S(1)} %fusion.15), slice={[0:1:1], [0:4:2], [0:16:2], [0:16:2], [0:512:1]} | slice | bytes 262144 | tf_op jit(solution)/shard_map/slice | solution.py:22
  77.1 5.0 %slice.320 = bf16[1,2,8,8,512]{4,3,2,1,0:T(8,128)(2,1)} slice(bf16[1,5,17,17,512]{4,3,2,1,0:T(8,128)(2,1)S(1)} %fusion.15), slice={[0:1:1], [0:4:2], [0:16:2], [2:17:2], [0:512:1]} | slice | bytes 262144 | tf_op jit(solution)/shard_map/slice | solution.py:22
  82.1 4.9 %slice.321 = bf16[1,2,8,8,512]{4,3,2,1,0:T(8,128)(2,1)} slice(bf16[1,5,17,17,512]{4,3,2,1,0:T(8,128)(2,1)S(1)} %fusion.15), slice={[0:1:1], [0:4:2], [1:17:2], [0:16:2], [0:512:1]} | slice | bytes 262144 | tf_op jit(solution)/shard_map/slice | solution.py:22
  87.0 4.9 %slice.322 = bf16[1,2,8,8,512]{4,3,2,1,0:T(8,128)(2,1)} slice(bf16[1,5,17,17,512]{4,3,2,1,0:T(8,128)(2,1)S(1)} %fusion.15), slice={[0:1:1], [0:4:2], [1:17:2], [1:17:2], [0:512:1]} | slice | bytes 262144 | tf_op jit(solution)/shard_map/slice | solution.py:22
  91.9 5.0 %slice.323 = bf16[1,2,8,8,512]{4,3,2,1,0:T(8,128)(2,1)} slice(bf16[1,5,17,17,512]{4,3,2,1,0:T(8,128)(2,1)S(1)} %fusion.15), slice={[0:1:1], [0:4:2], [1:17:2], [2:17:2], [0:512:1]} | slice | bytes 262144 | tf_op jit(solution)/shard_map/slice | solution.py:22
  96.9 5.0 %slice.324 = bf16[1,2,8,8,512]{4,3,2,1,0:T(8,128)(2,1)} slice(bf16[1,5,17,17,512]{4,3,2,1,0:T(8,128)(2,1)S(1)} %fusion.15), slice={[0:1:1], [0:4:2], [2:17:2], [0:16:2], [0:512:1]} | slice | bytes 262144 | tf_op jit(solution)/shard_map/slice | solution.py:22
  101.9 4.9 %slice.325 = bf16[1,2,8,8,512]{4,3,2,1,0:T(8,128)(2,1)} slice(bf16[1,5,17,17,512]{4,3,2,1,0:T(8,128)(2,1)S(1)} %fusion.15), slice={[0:1:1], [0:4:2], [2:17:2], [1:17:2], [0:512:1]} | slice | bytes 262144 | tf_op jit(solution)/shard_map/slice | solution.py:22
  106.8 5.0 %slice.326 = bf16[1,2,8,8,512]{4,3,2,1,0:T(8,128)(2,1)} slice(bf16[1,5,17,17,512]{4,3,2,1,0:T(8,128)(2,1)S(1)} %fusion.15), slice={[0:1:1], [0:4:2], [2:17:2], [2:17:2], [0:512:1]} | slice | bytes 262144 | tf_op jit(solution)/shard_map/slice | solution.py:22
  111.8 4.9 %slice.327 = bf16[1,2,8,8,512]{4,3,2,1,0:T(8,128)(2,1)} slice(bf16[1,5,17,17,512]{4,3,2,1,0:T(8,128)(2,1)S(1)} %fusion.15), slice={[0:1:1], [1:5:2], [0:16:2], [0:16:2], [0:512:1]} | slice | bytes 262144 | tf_op jit(solution)/shard_map/slice | solution.py:22
  116.7 4.9 %slice.328 = bf16[1,2,8,8,512]{4,3,2,1,0:T(8,128)(2,1)} slice(bf16[1,5,17,17,512]{4,3,2,1,0:T(8,128)(2,1)S(1)} %fusion.15), slice={[0:1:1], [1:5:2], [0:16:2], [1:17:2], [0:512:1]} | slice | bytes 262144 | tf_op jit(solution)/shard_map/slice | solution.py:22
  121.7 5.0 %slice.329 = bf16[1,2,8,8,512]{4,3,2,1,0:T(8,128)(2,1)} slice(bf16[1,5,17,17,512]{4,3,2,1,0:T(8,128)(2,1)S(1)} %fusion.15), slice={[0:1:1], [1:5:2], [0:16:2], [2:17:2], [0:512:1]} | slice | bytes 262144 | tf_op jit(solution)/shard_map/slice | solution.py:22
  131.5 4.9 %slice.331 = bf16[1,2,8,8,512]{4,3,2,1,0:T(8,128)(2,1)} slice(bf16[1,5,17,17,512]{4,3,2,1,0:T(8,128)(2,1)S(1)} %fusion.15), slice={[0:1:1], [1:5:2], [1:17:2], [1:17:2], [0:512:1]} | slice | bytes 262144 | tf_op jit(solution)/shard_map/slice | solution.py:22
  136.5 5.0 %slice.332 = bf16[1,2,8,8,512]{4,3,2,1,0:T(8,128)(2,1)} slice(bf16[1,5,17,17,512]{4,3,2,1,0:T(8,128)(2,1)S(1)} %fusion.15), slice={[0:1:1], [1:5:2], [1:17:2], [2:17:2], [0:512:1]} | slice | bytes 262144 | tf_op jit(solution)/shard_map/slice | solution.py:22
  141.4 4.9 %slice.333 = bf16[1,2,8,8,512]{4,3,2,1,0:T(8,128)(2,1)} slice(bf16[1,5,17,17,512]{4,3,2,1,0:T(8,128)(2,1)S(1)} %fusion.15), slice={[0:1:1], [1:5:2], [2:17:2], [0:16:2], [0:512:1]} | slice | bytes 262144 | tf_op jit(solution)/shard_map/slice | solution.py:22
  146.4 4.9 %slice.334 = bf16[1,2,8,8,512]{4,3,2,1,0:T(8,128)(2,1)} slice(bf16[1,5,17,17,512]{4,3,2,1,0:T(8,128)(2,1)S(1)} %fusion.15), slice={[0:1:1], [1:5:2], [2:17:2], [1:17:2], [0:512:1]} | slice | bytes 262144 | tf_op jit(solution)/shard_map/slice | solution.py:22
  151.3 5.0 %slice.335 = bf16[1,2,8,8,512]{4,3,2,1,0:T(8,128)(2,1)} slice(bf16[1,5,17,17,512]{4,3,2,1,0:T(8,128)(2,1)S(1)} %fusion.15), slice={[0:1:1], [1:5:2], [2:17:2], [2:17:2], [0:512:1]} | slice | bytes 262144 | tf_op jit(solution)/shard_map/slice | solution.py:22
  166.1 5.0 %slice.338 = bf16[1,2,8,8,512]{4,3,2,1,0:T(8,128)(2,1)} slice(bf16[1,5,17,17,512]{4,3,2,1,0:T(8,128)(2,1)S(1)} %fusion.15), slice={[0:1:1], [2:5:2], [0:16:2], [2:17:2], [0:512:1]} | slice | bytes 262144 | tf_op jit(solution)/shard_map/slice | solution.py:22
  171.1 4.9 %slice.339 = bf16[1,2,8,8,512]{4,3,2,1,0:T(8,128)(2,1)} slice(bf16[1,5,17,17,512]{4,3,2,1,0:T(8,128)(2,1)S(1)} %fusion.15), slice={[0:1:1], [2:5:2], [1:17:2], [0:16:2], [0:512:1]} | slice | bytes 262144 | tf_op jit(solution)/shard_map/slice | solution.py:22
  214.9 6.0 %copy.17 = bf16[128,13824]{0,1:T(8,128)(2,1)} copy(bf16[128,13824]{1,0:T(8,128)(2,1)} %bitcast) | data formatting | bytes 7077888 | tf_op jit(solution)/shard_map/reshape | solution.py:65
  239.2 143.1 %all-reduce.4.cloned.1.call-done = f32[2,27,512,32]{2,3,1,0:T(8,128)} async-done(((f32[2,27,512,32]{2,3,1,0:T(8,128)}), f32[2,27,512,32]{2,3,1,0:T(8,128)}) %all-reduce.4.cloned.1.call-update) | async-done | bytes 3538960 | tf_op jit(solution)/shard_map/psum | solution.py:100
  382.2 10.7 %fusion.11 = f32[2,27,512,32]{2,1,3,0:T(8,128)} fusion(f32[2,27,512,32]{2,3,1,0:T(8,128)} %all-reduce.4.cloned.1.call-done, f32[2,27,27,1]{2,0,1,3:T(2,128)S(1)} %bitcast.215), kind=kOutput, calls=%fused_computation.41 | convolution fusion | flops 286654464 | bytes 7083720 | tf_op jit(solution)/shard_map/lst,ltij->lsij/dot_general | solution.py:101
  393.0 10.1 %fusion.7 = f32[2,27,32,512]{3,2,1,0:T(8,128)S(1)} fusion(f32[2,27,512,32]{2,1,3,0:T(8,128)} %fusion.11, f32[2,512,512]{2,1,0:T(8,128)} %all-gather.2.cloned.1.call-done), kind=kOutput, calls=%fused_computation.37 | convolution fusion | flops 5435817984 | bytes 9175040 | tf_op jit(solution)/shard_map/lik,lskj->lsij/dot_general | solution.py:102
  406.9 73.8 %reduce-scatter.4.cloned.1.call-done = f32[32,864]{1,0:T(8,128)} async-done(((f32[512,864]{1,0:T(8,128)}), f32[32,864]{1,0:T(8,128)}) %reduce-scatter.4.cloned.1.call-update) | async-done | bytes 110608
  (214 shorter events, 133.4 us)
Async XLA Ops:
  7.4 3.1 copy-start
  7.4 55.8 %copy-start.2 = (bf16[27,512,32]{1,2,0:T(8,128)(2,1)S(1)}, bf16[27,512,32]{1,2,0:T(8,128)(2,1)}, u32[]{:S(2)}) copy-start(bf16[27,512,32]{1,2,0:T(8,128)(2,1)} %param.10) | copy-start | bytes 2654212
  7.4 374.9 %all-reduce.4.cloned.1.call-start = ((), (), s32[]{:S(2)}) async-start(), calls=%async_computation.1 | async-start | bytes 7077888 | tf_op jit(solution)/shard_map/psum | solution.py:100
  8.5 56.6 %collective-permute-start = (bf16[1,1,16,16,512]{4,3,2,1,0:T(8,128)(2,1)S(1)}, bf16[1,1,16,16,512]{4,3,2,1,0:T(8,128)(2,1)S(1)}, u32[]{:S(2)}, u32[]{:S(2)}) collective-permute-start(bf16[1,1,16,16,512]{4,3,2,1,0:T(8,128)(2,1)S(1)} %slice.317), channel_id=1, source_target_pairs={{0,1},{2,3},{4,5},{6,7},{8,9},{10,11},{12,13},{14,15},{16,17},{18,... | collective-permute-start | bytes 786440 | tf_op jit(solution)/shard_map/ppermute | solution.py:12
  55.4 9.4 %collective-permute-start.1 = (f32[1,1,8,8,32]{4,1,3,2,0:T(1,128)S(1)}, f32[1,1,8,8,32]{4,1,3,2,0:T(1,128)S(1)}, u32[]{:S(2)}, u32[]{:S(2)}) collective-permute-start(f32[1,1,8,8,32]{4,1,3,2,0:T(1,128)S(1)} %slice.702), channel_id=1, source_target_pairs={{1,0},{3,2},{5,4},{7,6},{9,8},{11,10},{13,12},{15,14},{17,16},{19,... | collective-permute-start | bytes 24584 | tf_op jit(solution)/shard_map/ppermute | solution.py:12
  183.7 22.4 %copy-start.11 = (bf16[1,2,8,8,512]{4,3,2,1,0:T(8,128)(2,1)S(1)}, bf16[1,2,8,8,512]{4,3,2,1,0:T(8,128)(2,1)}, u32[]{:S(2)}) copy-start(bf16[1,2,8,8,512]{4,3,2,1,0:T(8,128)(2,1)} %slice.332) | copy-start | bytes 393220
  183.7 23.1 %copy-start.10 = (bf16[1,2,8,8,512]{4,3,2,1,0:T(8,128)(2,1)S(1)}, bf16[1,2,8,8,512]{4,3,2,1,0:T(8,128)(2,1)}, u32[]{:S(2)}) copy-start(bf16[1,2,8,8,512]{4,3,2,1,0:T(8,128)(2,1)} %slice.333) | copy-start | bytes 393220
  183.7 23.7 %copy-start.9 = (bf16[1,2,8,8,512]{4,3,2,1,0:T(8,128)(2,1)S(1)}, bf16[1,2,8,8,512]{4,3,2,1,0:T(8,128)(2,1)}, u32[]{:S(2)}) copy-start(bf16[1,2,8,8,512]{4,3,2,1,0:T(8,128)(2,1)} %slice.334) | copy-start | bytes 393220
  183.7 24.4 %copy-start.8 = (bf16[1,2,8,8,512]{4,3,2,1,0:T(8,128)(2,1)S(1)}, bf16[1,2,8,8,512]{4,3,2,1,0:T(8,128)(2,1)}, u32[]{:S(2)}) copy-start(bf16[1,2,8,8,512]{4,3,2,1,0:T(8,128)(2,1)} %slice.335) | copy-start | bytes 393220
  183.7 25.1 %copy-start.7 = (bf16[1,2,8,8,512]{4,3,2,1,0:T(8,128)(2,1)S(1)}, bf16[1,2,8,8,512]{4,3,2,1,0:T(8,128)(2,1)}, u32[]{:S(2)}) copy-start(bf16[1,2,8,8,512]{4,3,2,1,0:T(8,128)(2,1)} %slice.336) | copy-start | bytes 393220
  183.7 25.8 %copy-start.6 = (bf16[1,2,8,8,512]{4,3,2,1,0:T(8,128)(2,1)S(1)}, bf16[1,2,8,8,512]{4,3,2,1,0:T(8,128)(2,1)}, u32[]{:S(2)}) copy-start(bf16[1,2,8,8,512]{4,3,2,1,0:T(8,128)(2,1)} %slice.337) | copy-start | bytes 393220
  183.7 26.4 %copy-start.5 = (bf16[1,2,8,8,512]{4,3,2,1,0:T(8,128)(2,1)S(1)}, bf16[1,2,8,8,512]{4,3,2,1,0:T(8,128)(2,1)}, u32[]{:S(2)}) copy-start(bf16[1,2,8,8,512]{4,3,2,1,0:T(8,128)(2,1)} %slice.338) | copy-start | bytes 393220
  183.7 27.1 %copy-start.4 = (bf16[1,2,8,8,512]{4,3,2,1,0:T(8,128)(2,1)S(1)}, bf16[1,2,8,8,512]{4,3,2,1,0:T(8,128)(2,1)}, u32[]{:S(2)}) copy-start(bf16[1,2,8,8,512]{4,3,2,1,0:T(8,128)(2,1)} %slice.339) | copy-start | bytes 393220
  183.7 27.7 %copy-start.3 = (bf16[1,2,8,8,512]{4,3,2,1,0:T(8,128)(2,1)S(1)}, bf16[1,2,8,8,512]{4,3,2,1,0:T(8,128)(2,1)}, u32[]{:S(2)}) copy-start(bf16[1,2,8,8,512]{4,3,2,1,0:T(8,128)(2,1)} %slice.340) | copy-start | bytes 393220
  214.9 6.0 %copy-start.1 = (bf16[27,4,8,512]{3,2,0,1:T(8,128)(2,1)S(1)}, bf16[27,4,8,512]{3,2,0,1:T(8,128)(2,1)}, u32[]{:S(2)}) copy-start(bf16[27,4,8,512]{3,2,0,1:T(8,128)(2,1)} %copy.34) | copy-start | bytes 2654212
  224.1 11.5 %copy-start.14 = (bf16[1,1,4,4,512]{4,3,2,1,0:T(4,128)(2,1)S(1)}, bf16[1,1,4,4,512]{4,3,2,1,0:T(4,128)(2,1)}, u32[]{:S(2)}) copy-start(bf16[1,1,4,4,512]{4,3,2,1,0:T(4,128)(2,1)} %param.12) | copy-start | bytes 49156
  224.3 7.1 %collective-permute-start.2 = (bf16[1,1,8,8,32]{4,3,2,1,0:T(8,128)(2,1)S(1)}, bf16[1,1,8,8,32]{4,3,2,1,0:T(8,128)(2,1)S(1)}, u32[]{:S(2)}, u32[]{:S(2)}) collective-permute-start(bf16[1,1,8,8,32]{4,3,2,1,0:T(8,128)(2,1)S(1)} %slice.703), channel_id=1, source_target_pairs={{0,1},{2,3},{4,5},{6,7},{8,9},{10,11},{12,13},{14,15},{16,17},{18,... | collective-permute-start | bytes 12296 | tf_op jit(solution)/shard_map/ppermute | solution.py:12
  238.3 143.9 %copy-start.12 = (f32[2,27,27]{2,0,1:T(2,128)S(1)}, f32[2,27,27]{2,0,1:T(2,128)}, u32[]{:S(2)}) copy-start(f32[2,27,27]{2,0,1:T(2,128)} %param.13) | copy-start | bytes 17500
  238.3 154.6 %all-gather.2.cloned.1.call-start = ((), (), s32[]{:S(2)}) async-start(), calls=%async_computation.2 | async-start | bytes 2228224 | tf_op jit(solution)/shard_map/all_gather | solution.py:104
  238.9 241.7 %reduce-scatter.4.cloned.1.call-start = ((), (), s32[]{:S(2)}) async-start(), calls=%async_computation.3 | async-start | bytes 1949696
  393.0 10.1 %copy-start.13 = (f32[2,32,16]{1,2,0:T(8,128)S(1)}, f32[2,32,16]{1,2,0:T(8,128)}, u32[]{:S(2)}) copy-start(f32[2,32,16]{1,2,0:T(8,128)} %param.15) | copy-start | bytes 12292
Sparse Core Ops, SparseCore 0:
  238.5 143.7 all-reduce.3
Sparse Core Ops, SparseCore 1:
  240.9 75.5 all-gather.1
  406.9 73.6 reduce-scatter.3
where the time goes:
time: 500 us; the launch traced here: 490 us
  waiting for transfers between devices  220 us (44%)
  local copies, waits for them, and re-layouts  166 us (33%)
  other arithmetic  45.8 us (9%)
  matrix products  30.9 us (6%)
  between operations  16 us (3%)
  starting transfers between devices  10.7 us (2%)
    psum x1, waiting for transfers between devices, shards(): summed = lax.psum(stacked, ('replica', 'tm'))  143 us
    slice x54, local copies, waits for them, and re-layouts, tap_patches(): padded[:, along_time:along_time + 2 * out_frames:2, along_rows:along_rows...  120 us
    unnamed x4, waiting for transfers between devices  74.3 us
    scatter-add x27, other arithmetic, spread_back(): total = total.at[:, along_time:along_time + 2 * out_frames:2, along_rows:...  40.8 us
    unnamed x58, local copies, waits for them, and re-layouts  33.9 us
    dot_general x1, matrix products, shards(): tap_mixed = jnp.einsum('lst,ltij->lsij', tap_mix, summed, precision=highest)  10.7 us
    ppermute x3, starting transfers between devices, shifted(): return lax.ppermute(block, axis, route)  10.4 us
    dot_general x1, matrix products, shards(): jnp.einsum('lik,lskj->lsij', lax.all_gather(left_panels, 'fsdp', axis=1,...  10.1 us
  transfers between devices with their start and end apart: 6, of which 4 were waited for; matrix products, arithmetic and copies ran while one was open for 12% of the time, Pallas kernels for 0%

commit v1 on v0

--- a/solution.py
+++ b/solution.py
@@ -2,8 +2,15 @@
 import jax.numpy as jnp
 from jax import lax
 from jax.sharding import PartitionSpec as P
+from jax.lax import psum
 
 TAPS = 27
+
+
+def group_the_racks(device_axis, shard_axis, chunk):
+    for p in (shard_axis, device_axis):
+        chunk = psum(chunk, p)
+    return chunk
 
 
 def shifted(block, axis, distance):
@@ -97,7 +104,7 @@
         TAPS, channels, own_width
     )
     stacked = jnp.stack([first_grad, second_grad])
-    summed = lax.psum(stacked, ("replica", "tm"))
+    summed = group_the_racks("replica", "tm", stacked)
     tap_mixed = jnp.einsum("lst,ltij->lsij", tap_mix, summed, precision=highest)
     left_done = jnp.einsum(
         "lik,lskj->lsij",

time: 500 us -> 623 us (1.25)
  the two profiles are of different devices: /device:TPU:4 before, /device:TPU:2 now
where the time goes in v1:
time: 623 us; the launch traced here: 613 us
  waiting for transfers between devices  347 us (56%)
  local copies, waits for them, and re-layouts  166 us (27%)
  other arithmetic  45.9 us (7%)
  matrix products  30.9 us (5%)
  between operations  16 us (3%)
  starting transfers between devices  7.29 us (1%)
    psum x2, waiting for transfers between devices, group_the_racks(): chunk = psum(chunk, p)  266 us
    slice x54, local copies, waits for them, and re-layouts, tap_patches(): padded[:, along_time:along_time + 2 * out_frames:2, along_rows:along_rows...  120 us
    unnamed x5, waiting for transfers between devices  75.6 us
    scatter-add x27, other arithmetic, spread_back(): total = total.at[:, along_time:along_time + 2 * out_frames:2, along_rows:...  40.8 us
    unnamed x58, local copies, waits for them, and re-layouts  33.9 us
  transfers between devices with their start and end apart: 7, of which 4 were waited for; matrix products, arithmetic and copies ran while one was open for 10% of the time, Pallas kernels for 0%

profile of v1, /device:TPU:2, one launch (start us, length us, event | category | flops | bytes accessed | tf_op | source)
XLA Modules:
  0.0 613.0 jit_solution(5589824426056030264)
XLA Ops:
  60.4 5.0 collective-permute-done.1
  67.9 5.0 slice.318
  77.8 5.0 slice.320
  82.8 4.9 slice.321
  87.7 4.9 slice.322
  92.7 5.0 slice.323
  97.6 5.0 slice.324
  102.6 4.9 slice.325
  107.5 5.0 slice.326
  112.5 4.9 slice.327
  117.4 4.9 slice.328
  122.4 5.0 slice.329
  137.2 5.0 slice.332
  142.1 4.9 slice.333
  147.1 4.9 slice.334
  152.0 5.0 slice.335
  166.8 5.0 slice.338
  171.8 4.9 slice.339
  215.6 6.0 copy.17
  237.0 121.3 %all-reduce.5.cloned.1.call-done = f32[2,27,512,32]{2,3,1,0:T(8,128)} async-done(((f32[2,27,512,32]{2,3,1,0:T(8,128)}), f32[2,27,512,32]{2,3,1,0:T(8,128)}) %all-reduce.5.cloned.1.call-update) | async-done | bytes 3538960 | tf_op jit(solution)/shard_map/psum | solution.py:12
  359.2 144.8 %all-reduce.7.cloned.1.call-done = f32[2,27,512,32]{2,3,1,0:T(8,128)} async-done(((f32[2,27,512,32]{2,3,1,0:T(8,128)}), f32[2,27,512,32]{2,3,1,0:T(8,128)}) %all-reduce.7.cloned.1.call-update) | async-done | bytes 3538960 | tf_op jit(solution)/shard_map/psum | solution.py:12
  504.0 10.7 %fusion.11 = f32[2,27,512,32]{2,1,3,0:T(8,128)} fusion(f32[2,27,512,32]{2,3,1,0:T(8,128)} %all-reduce.7.cloned.1.call-done, f32[2,27,27,1]{2,0,1,3:T(2,128)S(1)} %bitcast.215), kind=kOutput, calls=%fused_computation.41 | convolution fusion | flops 286654464 | bytes 7083720 | tf_op jit(solution)/shard_map/lst,ltij->lsij/dot_general | solution.py:108
  514.7 10.1 %fusion.7 = f32[2,27,32,512]{3,2,1,0:T(8,128)S(1)} fusion(f32[2,27,512,32]{2,1,3,0:T(8,128)} %fusion.11, f32[2,512,512]{2,1,0:T(8,128)} %all-gather.2.cloned.1.call-done), kind=kOutput, calls=%fused_computation.37 | convolution fusion | flops 5435817984 | bytes 9175040 | tf_op jit(solution)/shard_map/lik,lskj->lsij/dot_general | solution.py:109
  528.6 75.0 %reduce-scatter.4.cloned.1.call-done = f32[32,864]{1,0:T(8,128)} async-done(((f32[512,864]{1,0:T(8,128)}), f32[32,864]{1,0:T(8,128)}) %reduce-scatter.4.cloned.1.call-update) | async-done | bytes 110608
  (217 shorter events, 139.8 us)
Async XLA Ops:
  7.4 5.8 copy-start
  7.4 52.1 %copy-start.2 = (bf16[27,512,32]{1,2,0:T(8,128)(2,1)S(1)}, bf16[27,512,32]{1,2,0:T(8,128)(2,1)}, u32[]{:S(2)}) copy-start(bf16[27,512,32]{1,2,0:T(8,128)(2,1)} %param.10) | copy-start | bytes 2654212
  7.4 350.9 %all-reduce.5.cloned.1.call-start = ((), (), s32[]{:S(2)}) async-start(), calls=%async_computation.1 | async-start | bytes 7077888 | tf_op jit(solution)/shard_map/psum | solution.py:12
  8.5 57.3 %collective-permute-start = (bf16[1,1,16,16,512]{4,3,2,1,0:T(8,128)(2,1)S(1)}, bf16[1,1,16,16,512]{4,3,2,1,0:T(8,128)(2,1)S(1)}, u32[]{:S(2)}, u32[]{:S(2)}) collective-permute-start(bf16[1,1,16,16,512]{4,3,2,1,0:T(8,128)(2,1)S(1)} %slice.317), channel_id=1, source_target_pairs={{0,1},{2,3},{4,5},{6,7},{8,9},{10,11},{12,13},{14,15},{16,17},{18,... | collective-permute-start | bytes 786440 | tf_op jit(solution)/shard_map/ppermute | solution.py:19
  58.1 7.3 %collective-permute-start.1 = (f32[1,1,8,8,32]{4,1,3,2,0:T(1,128)S(1)}, f32[1,1,8,8,32]{4,1,3,2,0:T(1,128)S(1)}, u32[]{:S(2)}, u32[]{:S(2)}) collective-permute-start(f32[1,1,8,8,32]{4,1,3,2,0:T(1,128)S(1)} %slice.702), channel_id=1, source_target_pairs={{1,0},{3,2},{5,4},{7,6},{9,8},{11,10},{13,12},{15,14},{17,16},{19,... | collective-permute-start | bytes 24584 | tf_op jit(solution)/shard_map/ppermute | solution.py:19
  184.4 22.4 %copy-start.11 = (bf16[1,2,8,8,512]{4,3,2,1,0:T(8,128)(2,1)S(1)}, bf16[1,2,8,8,512]{4,3,2,1,0:T(8,128)(2,1)}, u32[]{:S(2)}) copy-start(bf16[1,2,8,8,512]{4,3,2,1,0:T(8,128)(2,1)} %slice.332) | copy-start | bytes 393220
  184.4 23.1 %copy-start.10 = (bf16[1,2,8,8,512]{4,3,2,1,0:T(8,128)(2,1)S(1)}, bf16[1,2,8,8,512]{4,3,2,1,0:T(8,128)(2,1)}, u32[]{:S(2)}) copy-start(bf16[1,2,8,8,512]{4,3,2,1,0:T(8,128)(2,1)} %slice.333) | copy-start | bytes 393220
  184.4 23.7 %copy-start.9 = (bf16[1,2,8,8,512]{4,3,2,1,0:T(8,128)(2,1)S(1)}, bf16[1,2,8,8,512]{4,3,2,1,0:T(8,128)(2,1)}, u32[]{:S(2)}) copy-start(bf16[1,2,8,8,512]{4,3,2,1,0:T(8,128)(2,1)} %slice.334) | copy-start | bytes 393220
  184.4 24.4 %copy-start.8 = (bf16[1,2,8,8,512]{4,3,2,1,0:T(8,128)(2,1)S(1)}, bf16[1,2,8,8,512]{4,3,2,1,0:T(8,128)(2,1)}, u32[]{:S(2)}) copy-start(bf16[1,2,8,8,512]{4,3,2,1,0:T(8,128)(2,1)} %slice.335) | copy-start | bytes 393220
  184.4 25.1 %copy-start.7 = (bf16[1,2,8,8,512]{4,3,2,1,0:T(8,128)(2,1)S(1)}, bf16[1,2,8,8,512]{4,3,2,1,0:T(8,128)(2,1)}, u32[]{:S(2)}) copy-start(bf16[1,2,8,8,512]{4,3,2,1,0:T(8,128)(2,1)} %slice.336) | copy-start | bytes 393220
  184.4 25.8 %copy-start.6 = (bf16[1,2,8,8,512]{4,3,2,1,0:T(8,128)(2,1)S(1)}, bf16[1,2,8,8,512]{4,3,2,1,0:T(8,128)(2,1)}, u32[]{:S(2)}) copy-start(bf16[1,2,8,8,512]{4,3,2,1,0:T(8,128)(2,1)} %slice.337) | copy-start | bytes 393220
  184.4 26.4 %copy-start.5 = (bf16[1,2,8,8,512]{4,3,2,1,0:T(8,128)(2,1)S(1)}, bf16[1,2,8,8,512]{4,3,2,1,0:T(8,128)(2,1)}, u32[]{:S(2)}) copy-start(bf16[1,2,8,8,512]{4,3,2,1,0:T(8,128)(2,1)} %slice.338) | copy-start | bytes 393220
  184.4 27.1 %copy-start.4 = (bf16[1,2,8,8,512]{4,3,2,1,0:T(8,128)(2,1)S(1)}, bf16[1,2,8,8,512]{4,3,2,1,0:T(8,128)(2,1)}, u32[]{:S(2)}) copy-start(bf16[1,2,8,8,512]{4,3,2,1,0:T(8,128)(2,1)} %slice.339) | copy-start | bytes 393220
  184.5 27.7 %copy-start.3 = (bf16[1,2,8,8,512]{4,3,2,1,0:T(8,128)(2,1)S(1)}, bf16[1,2,8,8,512]{4,3,2,1,0:T(8,128)(2,1)}, u32[]{:S(2)}) copy-start(bf16[1,2,8,8,512]{4,3,2,1,0:T(8,128)(2,1)} %slice.340) | copy-start | bytes 393220
  215.6 6.0 copy-start.1
  224.8 9.4 %copy-start.14 = (bf16[1,1,4,4,512]{4,3,2,1,0:T(4,128)(2,1)S(1)}, bf16[1,1,4,4,512]{4,3,2,1,0:T(4,128)(2,1)}, u32[]{:S(2)}) copy-start(bf16[1,1,4,4,512]{4,3,2,1,0:T(4,128)(2,1)} %param.12) | copy-start | bytes 49156
  225.0 4.9 collective-permute-start.2
  236.9 267.1 %copy-start.12 = (f32[2,27,27]{2,0,1:T(2,128)S(1)}, f32[2,27,27]{2,0,1:T(2,128)}, u32[]{:S(2)}) copy-start(f32[2,27,27]{2,0,1:T(2,128)} %param.13) | copy-start | bytes 17500
  236.9 267.1 %all-reduce.7.cloned.1.call-start = ((), (), s32[]{:S(2)}) async-start(), calls=%async_computation.2 | async-start | bytes 7077888 | tf_op jit(solution)/shard_map/psum | solution.py:12
  358.3 156.4 %all-gather.2.cloned.1.call-start = ((), (), s32[]{:S(2)}) async-start(), calls=%async_computation.3 | async-start | bytes 2228224 | tf_op jit(solution)/shard_map/all_gather | solution.py:111
  358.9 244.7 %reduce-scatter.4.cloned.1.call-start = ((), (), s32[]{:S(2)}) async-start(), calls=%async_computation.4 | async-start | bytes 1949696
  514.7 10.1 %copy-start.13 = (f32[2,32,16]{1,2,0:T(8,128)S(1)}, f32[2,32,16]{1,2,0:T(8,128)}, u32[]{:S(2)}) copy-start(f32[2,32,16]{1,2,0:T(8,128)} %param.15) | copy-start | bytes 12292
Sparse Core Ops, SparseCore 0:
  237.0 121.2 all-reduce.4
  361.3 142.6 all-reduce.6
Sparse Core Ops, SparseCore 1:
  360.9 73.3 all-gather.1
  528.7 74.9 reduce-scatter.3
